TPU v7x, 32 devices: a whole 2x2x4 slice. The times are simulated.
32 devices in a mesh: seq: 16 (over z, y, x), mdl: 2 (over core).
Axes of the slice: x: 2, y: 2, z: 4, core: 2. Of those that a mesh axis runs over, the one named last changes fastest.
Arguments:
- hidden_in: bfloat16 [32, 4, 2048], P(None, None, 'seq'), may hold values from -25 to 25
- cache_keys: bfloat16 [32, 512, 2048], P(None, 'seq', 'mdl'), may hold values from -250 to 250, as said below
- cache_values: bfloat16 [32, 512, 2048], P(None, 'seq', 'mdl'), may hold values from -6 to 6
- lengths: int32 [32], replicated, may hold values from 1 to 508, as said below
- query_weight: bfloat16 [2048, 2048], P('seq', 'mdl'), may hold values from -0.125 to 0.125
- key_weight: bfloat16 [2048, 2048], P('seq', 'mdl'), may hold values from -0.125 to 0.125
- value_weight: bfloat16 [2048, 2048], P('seq', 'mdl'), may hold values from -0.125 to 0.125
- out_weight: bfloat16 [2048, 2048], P('mdl', 'seq'), may hold values from -0.125 to 0.125
- gate_weight: bfloat16 [2048, 8192], P('seq', 'mdl'), may hold values from -0.125 to 0.125
- up_weight: bfloat16 [2048, 8192], P('seq', 'mdl'), may hold values from -0.125 to 0.125
- down_weight: bfloat16 [8192, 2048], P('mdl', 'seq'), may hold values from -0.0625 to 0.0625
Outputs:
- hidden_out: bfloat16 [32, 4, 2048], P(None, None, 'seq')
- new_cache_keys: bfloat16 [32, 512, 2048], P(None, 'seq', 'mdl')
- new_cache_values: bfloat16 [32, 512, 2048], P(None, 'seq', 'mdl')
Inputs may be any that keep to these rules, and one draw needn't show every extreme that they name: `cache_keys`: keys are stored after their rotary embedding. `lengths`: at least one request has exactly 508 cached positions.
All inputs are finite; a program needn't handle non-finite values.
Results may differ from a plain program's by a relative error of at most 0.012.
The roundings to bfloat16 on the way count: a program that leaves them out, or rounds other values in their place, can miss the bound.
Values may be sent and summed in bfloat16 or wider, within the bound.
A program may use at most 64 MiB of HBM per device.

v0:
```python
import math
import jax
import jax.numpy as jnp
from jax import lax
from jax.sharding import PartitionSpec as P

D = 2048
HEADS = 16
EPS = 1e-05
THETA = 10000.0
NEGATIVE = -1e30


def rotate(vectors, placed_pos):
    head_size = vectors.shape[-1]
    half_dim = head_size // 2
    freqs = THETA ** (-jnp.arange(half_dim, dtype=jnp.float32) * 2.0 / head_size)
    angles = placed_pos.astype(jnp.float32)[..., None, None] * freqs
    cosine = jnp.cos(angles)
    sine = jnp.sin(angles)
    first_half = vectors[..., :half_dim]
    second_half = vectors[..., half_dim:]
    return jnp.concatenate(
        [first_half * cosine - second_half * sine, second_half * cosine + first_half * sine],
        axis=-1,
    )


def normalize(widened, row_sums, square_sums):
    row_mean = row_sums / D
    second_moment = square_sums / D
    inverse = 1.0 / jnp.sqrt(second_moment - row_mean * row_mean + EPS)
    return ((widened - row_mean[..., None]) * inverse[..., None]).astype(jnp.bfloat16)


def body(
    hidden_in,
    cache_keys,
    cache_values,
    lengths,
    query_weight,
    key_weight,
    value_weight,
    out_weight,
    gate_weight,
    up_weight,
    down_weight,
):
    requests, token_count, narrow_width = hidden_in.shape
    slot_count = cache_keys.shape[1]
    local_width = cache_keys.shape[2]
    head_size = D // HEADS
    local_heads = local_width // head_size
    score_scale = 1.0 / math.sqrt(head_size)
    shard_index = lax.axis_index("seq")
    slot_ids = shard_index * slot_count + jnp.arange(slot_count, dtype=jnp.int32)
    live_slots = slot_ids[None, :] < lengths[:, None]
    old_keys = cache_keys.reshape(requests, slot_count, local_heads, head_size)
    old_values = cache_values.reshape(requests, slot_count, local_heads, head_size).astype(
        jnp.float32
    )
    positions = lengths[:, None] + jnp.arange(token_count, dtype=jnp.int32)[None, :]
    out_list = []
    key_list = []
    value_list = []
    for token_step in range(1):
        row_block = hidden_in
        block_rows = row_block.shape[1]
        widened = row_block.astype(jnp.float32)
        row_sums, square_sums = lax.psum(
            (jnp.sum(widened, axis=-1), jnp.sum(widened * widened, axis=-1)), "seq"
        )
        normed = normalize(widened, row_sums, square_sums)
        query_part = jnp.einsum(
            "rnc,cm->rnm", normed, query_weight, preferred_element_type=jnp.float32
        )
        key_part = jnp.einsum("rnc,cm->rnm", normed, key_weight, preferred_element_type=jnp.float32)
        value_part = jnp.einsum(
            "rnc,cm->rnm", normed, value_weight, preferred_element_type=jnp.float32
        )
        queries, keys_full, values_full = lax.psum((query_part, key_part, value_part), "seq")
        placed_pos = positions[:, token_step : token_step + block_rows]
        queries = rotate(
            queries.reshape(requests, block_rows, local_heads, head_size), placed_pos
        ).astype(jnp.bfloat16)
        new_key = rotate(
            keys_full.reshape(requests, block_rows, local_heads, head_size), placed_pos
        ).astype(jnp.bfloat16)
        new_value = values_full.reshape(requests, block_rows, local_heads, head_size).astype(
            jnp.bfloat16
        )
        keys_new = jnp.concatenate(key_list + [new_key], axis=1)
        values_new = jnp.concatenate(value_list + [new_value], axis=1)
        old_scores = (
            jnp.einsum("rnhd,rjhd->rnhj", queries, old_keys, preferred_element_type=jnp.float32)
            * score_scale
        )
        old_scores = jnp.where(live_slots[:, None, None, :], old_scores, NEGATIVE)
        top_old = jnp.max(old_scores, axis=-1)
        weights_old = jnp.where(
            live_slots[:, None, None, :], jnp.exp(old_scores - top_old[..., None]), 0.0
        )
        total_old = jnp.sum(weights_old, axis=-1)
        summed_old = jnp.einsum(
            "rnhj,rjhd->rnhd", weights_old, old_values, precision=lax.Precision.HIGHEST
        )
        top_cache = lax.pmax(top_old, "seq")
        factor_old = jnp.exp(top_old - top_cache)
        total_cache, summed_cache = lax.psum(
            (total_old * factor_old, summed_old * factor_old[..., None]), "seq"
        )
        new_scores = (
            jnp.einsum("rnhd,rshd->rnhs", queries, keys_new, preferred_element_type=jnp.float32)
            * score_scale
        )
        key_index = jnp.arange(keys_new.shape[1], dtype=jnp.int32)
        query_index = token_step + jnp.arange(block_rows, dtype=jnp.int32)
        allowed = key_index[None, :] <= query_index[:, None]
        new_scores = jnp.where(allowed[None, :, None, :], new_scores, NEGATIVE)
        top_new = jnp.max(new_scores, axis=-1)
        weights_new = jnp.exp(new_scores - top_new[..., None])
        total_new = jnp.sum(weights_new, axis=-1)
        summed_new = jnp.einsum(
            "rnhs,rshd->rnhd",
            weights_new,
            values_new.astype(jnp.float32),
            precision=lax.Precision.HIGHEST,
        )
        top_score = jnp.maximum(top_cache, top_new)
        factor_cache = jnp.exp(top_cache - top_score)
        factor_new = jnp.exp(top_new - top_score)
        running = total_cache * factor_cache + total_new * factor_new
        combined = summed_cache * factor_cache[..., None] + summed_new * factor_new[..., None]
        attended = (
            (combined / running[..., None])
            .astype(jnp.bfloat16)
            .reshape(requests, block_rows, local_width)
        )
        attn_part = jnp.einsum(
            "rnm,mc->rnc", attended, out_weight, preferred_element_type=jnp.float32
        )
        mixed = widened + lax.psum(attn_part, "mdl")
        sums_mixed, squares_mixed = lax.psum(
            (jnp.sum(mixed, axis=-1), jnp.sum(mixed * mixed, axis=-1)), "seq"
        )
        normed2 = normalize(mixed, sums_mixed, squares_mixed)
        gate_part = jnp.einsum(
            "rnc,cf->rnf", normed2, gate_weight, preferred_element_type=jnp.float32
        )
        up_part = jnp.einsum("rnc,cf->rnf", normed2, up_weight, preferred_element_type=jnp.float32)
        gate_full, up_full = lax.psum((gate_part, up_part), "seq")
        act_full = (jax.nn.silu(gate_full) * up_full).astype(jnp.bfloat16)
        down_part = jnp.einsum(
            "rnf,fc->rnc", act_full, down_weight, preferred_element_type=jnp.float32
        )
        block_out = (mixed + lax.psum(down_part, "mdl")).astype(jnp.bfloat16)
        block_out, new_key, new_value = (block_out, new_key, new_value)
        out_list.append(block_out)
        key_list.append(new_key)
        value_list.append(new_value)
    hidden_out = jnp.concatenate(out_list, axis=1)
    keys_all = jnp.concatenate(key_list, axis=1)
    values_all = jnp.concatenate(value_list, axis=1)
    slot_hits = slot_ids[None, None, :] == positions[:, :, None]
    one_hot = slot_hits.astype(jnp.bfloat16)
    written = jnp.any(slot_hits, axis=1)[..., None]
    placed_keys = jnp.einsum(
        "rts,rtm->rsm",
        one_hot,
        keys_all.reshape(requests, token_count, local_width),
        preferred_element_type=jnp.float32,
    ).astype(jnp.bfloat16)
    placed_values = jnp.einsum(
        "rts,rtm->rsm",
        one_hot,
        values_all.reshape(requests, token_count, local_width),
        preferred_element_type=jnp.float32,
    ).astype(jnp.bfloat16)
    new_cache_keys = jnp.where(written, placed_keys, cache_keys)
    new_cache_values = jnp.where(written, placed_values, cache_values)
    return (hidden_out, new_cache_keys, new_cache_values)


def solution(mesh):
    placed = (
        P(None, None, "seq"),
        P(None, "seq", "mdl"),
        P(None, "seq", "mdl"),
        P(),
        P("seq", "mdl"),
        P("seq", "mdl"),
        P("seq", "mdl"),
        P("mdl", "seq"),
        P("seq", "mdl"),
        P("seq", "mdl"),
        P("mdl", "seq"),
    )
    return jax.shard_map(
        body,
        mesh=mesh,
        in_specs=placed,
        out_specs=(P(None, None, "seq"), P(None, "seq", "mdl"), P(None, "seq", "mdl")),
        check_vma=False,
    )
```

profile of v0, /device:TPU:0, one launch (start us, length us, event | category | flops | bytes accessed | tf_op | source)
XLA Modules:
  0.0 622.2 jit_solution(543046160231867355)
XLA Ops:
  8.2 43.5 %all-reduce.2 = (f32[32,4]{0,1:T(4,128)S(1)}, f32[32,4]{0,1:T(4,128)S(1)}) all-reduce(f32[32,4]{0,1:T(4,128)S(1)} %get-tuple-element.12, f32[32,4]{0,1:T(4,128)S(1)} %get-tuple-element.11), channel_id=1, replica_groups=mesh['seq'=16,'mdl'=2] {'seq'}, use_global_device_ids=true, to_apply=%region_3.0 | all-reduce | flops 256 | bytes 2048 | tf_op jit(solution)/shard_map/psum | solution.py:70
  51.7 1.2 fusion.42
  56.5 102.0 %all-reduce.12.cloned.1.call-done = f32[32,4,8,128]{3,1,2,0:T(4,128)} async-done(((f32[32,4,8,128]{3,1,2,0:T(4,128)}), f32[32,4,8,128]{3,1,2,0:T(4,128)}) %all-reduce.12.cloned.1.call-update) | async-done | bytes 524304 | tf_op jit(solution)/shard_map/psum | solution.py:81
  158.5 1.7 subtract_convert_fusion
  160.3 4.0 fusion.71
  164.2 75.7 %pmax.7 = f32[32,4,8]{1,2,0:T(8,128)S(1)} all-reduce(f32[32,4,8]{1,2,0:T(8,128)S(1)} %get-tuple-element.40), channel_id=1, replica_groups=mesh['seq'=16,'mdl'=2] {'seq'}, use_global_device_ids=true, to_apply=%region_6.0 | all-reduce | flops 1024 | bytes 8192 | tf_op jit(solution)/shard_map/pmax | solution.py:107
  240.0 1.7 fusion.34
  242.4 3.7 fusion.9
  246.2 1.3 fusion.38
  247.4 82.0 %all-reduce.21 = (bf16[32,4,1024]{2,0,1:T(8,128)(2,1)S(1)}, f32[32,4,8]{1,2,0:T(8,128)S(1)}) all-reduce(f32[32,4,1024]{2,0,1:T(8,128)S(1)} %fusion.38, f32[32,4,8]{1,2,0:T(8,128)} %get-tuple-element.26), channel_id=1, replica_groups=mesh['seq'=16,'mdl'=2] {'seq'}, use_global_device_ids=true, to_apply=%region_10.11 | all-reduce | flops 132096 | bytes 794624 | tf_op jit(solution)/shard_map/psum | solution.py:81
  329.5 27.1 %all-reduce.20.cloned.1.call-done = (f32[32,4,8,128]{3,1,2,0:T(4,128)}, f32[32,4,8,128]{3,1,2,0:T(4,128)}) async-done(((f32[32,4,8,128]{3,1,2,0:T(4,128)}, f32[32,4,8,128]{3,1,2,0:T(4,128)}), (f32[32,4,8,128]{3,1,2,0:T(4,128)}, f32[32,4,8,128]{3,1,2,0:T(4,128)})) %all-reduce.20.cloned.1.call-update) | async-done | bytes 1048592 | tf_op jit(solution)/shard_map/psum | solution.py:109
  356.7 1.7 multiply_subtract_fusion
  358.4 2.1 fusion.72
  361.1 2.1 fusion.26
  364.3 16.7 %all-reduce.14.cloned.1.call-done = f32[32,4,128]{2,0,1:T(8,128)} async-done(((f32[32,4,128]{2,0,1:T(8,128)}), f32[32,4,128]{2,0,1:T(8,128)}) %all-reduce.14.cloned.1.call-update) | async-done | bytes 65552 | tf_op jit(solution)/shard_map/psum | solution.py:142
  382.0 42.0 %all-reduce = (f32[32,4]{0,1:T(4,128)S(1)}, f32[32,4]{0,1:T(4,128)S(1)}) all-reduce(f32[32,4]{0,1:T(4,128)S(1)} %get-tuple-element.10, f32[32,4]{0,1:T(4,128)S(1)} %get-tuple-element.9), channel_id=1, replica_groups=mesh['seq'=16,'mdl'=2] {'seq'}, use_global_device_ids=true, to_apply=%region_18.19 | all-reduce | flops 256 | bytes 2048 | tf_op jit(solution)/shard_map/psum | solution.py:143
  424.0 2.6 fusion.29
  426.6 1.8 fusion.31
  428.6 1.5 copy-done.3
  430.1 3.6 convert_select_fusion
  433.7 159.6 %all-reduce.18.cloned.1.call-done = (f32[32,4,4096]{2,0,1:T(8,128)}, f32[32,4,4096]{2,0,1:T(8,128)}) async-done(((f32[32,4,4096]{2,0,1:T(8,128)}, f32[32,4,4096]{2,0,1:T(8,128)}), (f32[32,4,4096]{2,0,1:T(8,128)}, f32[32,4,4096]{2,0,1:T(8,128)})) %all-reduce.18.cloned.1.call-update) | async-done | bytes 4194320 | tf_op jit(solution)/shard_map/psum | solution.py:151
  593.3 4.0 fusion.27
  597.3 3.5 convert_select_fusion.1
  600.8 13.3 %all-reduce.16.cloned.1.call-done = f32[32,4,128]{2,0,1:T(8,128)} async-done(((f32[32,4,128]{2,0,1:T(8,128)}), f32[32,4,128]{2,0,1:T(8,128)}) %all-reduce.16.cloned.1.call-update) | async-done | bytes 65552 | tf_op jit(solution)/shard_map/psum | solution.py:156
  (74 shorter events, 9.7 us)
Async XLA Ops:
  7.2 416.8 %copy-start = (bf16[128,4096]{1,0:T(8,128)(2,1)S(1)}, bf16[128,4096]{1,0:T(8,128)(2,1)}, u32[]{:S(2)}) copy-start(bf16[128,4096]{1,0:T(8,128)(2,1)} %param.20) | copy-start | bytes 3145732
  7.2 47.1 %copy-start.1 = (bf16[32,4,128]{2,1,0:T(4,128)(2,1)S(1)}, bf16[32,4,128]{2,1,0:T(4,128)(2,1)}, u32[]{:S(2)}) copy-start(bf16[32,4,128]{2,1,0:T(4,128)(2,1)} %param.11) | copy-start | bytes 98308
  7.2 47.1 %copy-start.13 = (bf16[128,1024]{1,0:T(8,128)(2,1)S(1)}, bf16[128,1024]{1,0:T(8,128)(2,1)}, u32[]{:S(2)}) copy-start(bf16[128,1024]{1,0:T(8,128)(2,1)} %param.16) | copy-start | bytes 786436
  7.2 151.3 %all-reduce.12.cloned.1.call-start = ((), (), s32[]{:S(2)}) async-start(), calls=%async_computation | async-start | bytes 1048576 | tf_op jit(solution)/shard_map/psum | solution.py:81
  53.1 2.8 copy-start.18
  54.2 302.4 %all-reduce.20.cloned.1.call-start = ((), (), s32[]{:S(2)}) async-start(), calls=%async_computation.4 | async-start | bytes 2097152 | tf_op jit(solution)/shard_map/psum | solution.py:109
  56.5 107.7 %copy-start.9 = (f32[32,4,64]{2,1,0:T(4,128)}, f32[32,4,64]{2,1,0:T(4,128)S(1)}, u32[]{:S(2)}) copy-start(f32[32,4,64]{2,1,0:T(4,128)S(1)} %get-tuple-element.32) | copy-start | bytes 98308
  56.5 107.7 %copy-start.11 = (f32[32,4,64]{2,1,0:T(4,128)}, f32[32,4,64]{2,1,0:T(4,128)S(1)}, u32[]{:S(2)}) copy-start(f32[32,4,64]{2,1,0:T(4,128)S(1)} %get-tuple-element.33) | copy-start | bytes 98308
  160.2 4.0 copy-start.15
  160.2 4.0 copy-start.17
  160.3 82.1 %copy-start.2 = (bf16[32,32,1024]{2,1,0:T(8,128)(2,1)S(1)}, bf16[32,32,1024]{2,1,0:T(8,128)(2,1)}, u32[]{:S(2)}) copy-start(bf16[32,32,1024]{2,1,0:T(8,128)(2,1)} %param.13) | copy-start | bytes 6291460
  246.1 110.6 %copy-start.10 = (f32[32,4,64]{2,1,0:T(4,128)S(1)}, f32[32,4,64]{2,1,0:T(4,128)}, u32[]{:S(2)}) copy-start(f32[32,4,64]{2,1,0:T(4,128)} %copy-done.9) | copy-start | bytes 98308
  246.1 110.6 %copy-start.12 = (f32[32,4,64]{2,1,0:T(4,128)S(1)}, f32[32,4,64]{2,1,0:T(4,128)}, u32[]{:S(2)}) copy-start(f32[32,4,64]{2,1,0:T(4,128)} %copy-done.11) | copy-start | bytes 98308
  246.1 112.3 %copy-start.16 = (bf16[32,4,8,64]{3,1,2,0:T(4,128)(2,1)S(1)}, bf16[32,4,8,64]{3,1,2,0:T(4,128)(2,1)}, u32[]{:S(2)}) copy-start(bf16[32,4,8,64]{3,1,2,0:T(4,128)(2,1)} %copy-done.15) | copy-start | bytes 393220
  246.1 134.9 %all-reduce.14.cloned.1.call-start = ((), (), s32[]{:S(2)}) async-start(), calls=%async_computation.1 | async-start | bytes 131072 | tf_op jit(solution)/shard_map/psum | solution.py:142
  329.5 33.6 %copy-start.8 = (bf16[32,4,1024]{2,0,1:T(8,128)(2,1)}, bf16[32,4,1024]{2,0,1:T(8,128)(2,1)S(1)}, u32[]{:S(2)}) copy-start(bf16[32,4,1024]{2,0,1:T(8,128)(2,1)S(1)} %get-tuple-element.15) | copy-start | bytes 786436
  358.4 4.8 copy-start.7
  358.4 2.7 copy-start.19
  361.1 2.3 copy-start.14
  363.3 63.3 %copy-start.6 = (bf16[128,4096]{1,0:T(8,128)(2,1)S(1)}, bf16[128,4096]{1,0:T(8,128)(2,1)}, u32[]{:S(2)}) copy-start(bf16[128,4096]{1,0:T(8,128)(2,1)} %param.19) | copy-start | bytes 3145732
  364.2 229.1 %all-reduce.18.cloned.1.call-start = ((), (), s32[]{:S(2)}) async-start(), calls=%async_computation.3 | async-start | bytes 8388608 | tf_op jit(solution)/shard_map/psum | solution.py:151
  381.0 45.7 %copy-start.5 = (f32[32,4,128]{2,0,1:T(8,128)S(1)}, f32[32,4,128]{2,0,1:T(8,128)}, u32[]{:S(2)}) copy-start(f32[32,4,128]{2,0,1:T(8,128)} %all-reduce.14.cloned.1.call-done) | copy-start | bytes 196612
  428.5 185.7 %all-reduce.16.cloned.1.call-start = ((), (), s32[]{:S(2)}) async-start(), calls=%async_computation.2 | async-start | bytes 131072 | tf_op jit(solution)/shard_map/psum | solution.py:156
  593.3 4.0 copy-start.4
  (1 other events, 1.7 us)
Sparse Core Ops, SparseCore 0:
  54.3 104.1 all-reduce.11
  246.2 110.4 all-reduce.19
  364.3 16.5 all-reduce.13
  428.6 164.7 all-reduce.17
  597.4 16.6 all-reduce.15
where the time goes:
time: 623 us; the launch traced here: 622 us
  waiting for transfers between devices  319 us (51%)
  blocking collectives  243 us (39%)
  matrix products  31 us (5%)
  between operations  14.1 us (2%)
  other arithmetic  9.96 us (2%)
    psum x1, waiting for transfers between devices, body(): gate_full, up_full = lax.psum((gate_part, up_part), 'seq')  160 us
    psum x1, waiting for transfers between devices, body(): lax.psum((query_part, key_part, value_part), 'seq')  102 us
    psum x1, blocking collectives, body(): lax.psum((query_part, key_part, value_part), 'seq')  82 us
    pmax x1, blocking collectives, body(): top_cache = lax.pmax(top_old, 'seq')  75.7 us
    psum x1, blocking collectives, body(): lax.psum((jnp.sum(widened, axis=-1), jnp.sum(widened * widened, axis=-1))...  43.5 us
    psum x1, blocking collectives, body(): lax.psum((jnp.sum(mixed, axis=-1), jnp.sum(mixed * mixed, axis=-1)), 'seq')  42 us
    psum x1, waiting for transfers between devices, body(): lax.psum((total_old * factor_old, summed_old * factor_old[..., None]), 's...  27.1 us
    psum x1, waiting for transfers between devices, body(): mixed = widened + lax.psum(attn_part, 'mdl')  16.7 us
  transfers between devices with their start and end apart: 5, of which 5 were waited for; matrix products, arithmetic and copies ran while one was open for 2% of the time, Pallas kernels for 0%

commit v1 on v0

--- a/solution.py
+++ b/solution.py
@@ -153,7 +153,7 @@
         down_part = jnp.einsum(
             "rnf,fc->rnc", act_full, down_weight, preferred_element_type=jnp.float32
         )
-        block_out = (mixed + lax.psum(down_part, "mdl")).astype(jnp.bfloat16)
+        block_out = (mixed + jnp.sum(lax.all_gather(down_part, "mdl"), axis=0)).astype(jnp.bfloat16)
         block_out, new_key, new_value = (block_out, new_key, new_value)
         out_list.append(block_out)
         key_list.append(new_key)

time: 623 us -> 606 us (0.973)
  waiting for transfers between devices: 319 us -> 303 us
    psum x1 -> x0, waiting for transfers between devices: 13.3 us -> none  [body(): block_out = (mixed + lax.psum(down_part, 'mdl')).astype(jnp.bfloat16)]
  transfers between devices with their start and end apart: 5 -> 4, of which waited for: 5 -> 4; matrix products, arithmetic and copies ran while one was open for 2% -> 2% of each run, Pallas kernels for 0% -> 0%
where the time goes in v1:
time: 606 us; the launch traced here: 605 us
  waiting for transfers between devices  303 us (50%)
  blocking collectives  245 us (40%)
  matrix products  29.2 us (5%)
  between operations  14.1 us (2%)
  other arithmetic  9.12 us (2%)
    psum x1, waiting for transfers between devices, body(): gate_full, up_full = lax.psum((gate_part, up_part), 'seq')  157 us
    psum x1, waiting for transfers between devices, body(): lax.psum((query_part, key_part, value_part), 'seq')  102 us
    psum x1, blocking collectives, body(): lax.psum((query_part, key_part, value_part), 'seq')  82 us
    pmax x1, blocking collectives, body(): top_cache = lax.pmax(top_old, 'seq')  75.7 us
    psum x1, blocking collectives, body(): lax.psum((jnp.sum(widened, axis=-1), jnp.sum(widened * widened, axis=-1))...  43.5 us
    psum x1, blocking collectives, body(): lax.psum((jnp.sum(mixed, axis=-1), jnp.sum(mixed * mixed, axis=-1)), 'seq')  42 us
    psum x1, waiting for transfers between devices, body(): lax.psum((total_old * factor_old, summed_old * factor_old[..., None]), 's...  27 us
    psum x1, waiting for transfers between devices, body(): mixed = widened + lax.psum(attn_part, 'mdl')  16.7 us
  transfers between devices with their start and end apart: 4, of which 4 were waited for; matrix products, arithmetic and copies ran while one was open for 2% of the time, Pallas kernels for 0%

profile of v1, /device:TPU:0, one launch (start us, length us, event | category | flops | bytes accessed | tf_op | source)
XLA Modules:
  0.0 605.3 jit_solution(7110718772699935229)
XLA Ops:
  8.2 43.5 %all-reduce.2 = (f32[32,4]{0,1:T(4,128)S(1)}, f32[32,4]{0,1:T(4,128)S(1)}) all-reduce(f32[32,4]{0,1:T(4,128)S(1)} %get-tuple-element.12, f32[32,4]{0,1:T(4,128)S(1)} %get-tuple-element.11), channel_id=1, replica_groups=mesh['seq'=16,'mdl'=2] {'seq'}, use_global_device_ids=true, to_apply=%region_3.0 | all-reduce | flops 256 | bytes 2048 | tf_op jit(solution)/shard_map/psum | solution.py:70
  51.7 1.2 fusion.42
  56.5 102.0 %all-reduce.11.cloned.1.call-done = f32[32,4,8,128]{3,1,2,0:T(4,128)} async-done(((f32[32,4,8,128]{3,1,2,0:T(4,128)}), f32[32,4,8,128]{3,1,2,0:T(4,128)}) %all-reduce.11.cloned.1.call-update) | async-done | bytes 524304 | tf_op jit(solution)/shard_map/psum | solution.py:81
  158.5 1.7 subtract_convert_fusion
  160.3 4.0 fusion.71
  164.2 75.7 %pmax.7 = f32[32,4,8]{1,2,0:T(8,128)S(1)} all-reduce(f32[32,4,8]{1,2,0:T(8,128)S(1)} %get-tuple-element.40), channel_id=1, replica_groups=mesh['seq'=16,'mdl'=2] {'seq'}, use_global_device_ids=true, to_apply=%region_6.0 | all-reduce | flops 1024 | bytes 8192 | tf_op jit(solution)/shard_map/pmax | solution.py:107
  240.0 1.7 fusion.34
  242.4 3.7 fusion.9
  246.2 1.3 fusion.38
  247.4 82.0 %all-reduce.18 = (bf16[32,4,1024]{2,0,1:T(8,128)(2,1)S(1)}, f32[32,4,8]{1,2,0:T(8,128)S(1)}) all-reduce(f32[32,4,1024]{2,0,1:T(8,128)S(1)} %fusion.38, f32[32,4,8]{1,2,0:T(8,128)} %get-tuple-element.26), channel_id=1, replica_groups=mesh['seq'=16,'mdl'=2] {'seq'}, use_global_device_ids=true, to_apply=%region_10.11 | all-reduce | flops 132096 | bytes 794624 | tf_op jit(solution)/shard_map/psum | solution.py:81
  329.5 27.0 %all-reduce.17.cloned.1.call-done = (f32[32,4,8,128]{3,1,2,0:T(4,128)}, f32[32,4,8,128]{3,1,2,0:T(4,128)}) async-done(((f32[32,4,8,128]{3,1,2,0:T(4,128)}, f32[32,4,8,128]{3,1,2,0:T(4,128)}), (f32[32,4,8,128]{3,1,2,0:T(4,128)}, f32[32,4,8,128]{3,1,2,0:T(4,128)})) %all-reduce.17.cloned.1.call-update) | async-done | bytes 1048592 | tf_op jit(solution)/shard_map/psum | solution.py:109
  356.6 1.7 multiply_subtract_fusion
  358.3 2.1 fusion.72
  361.0 2.1 fusion.26
  364.1 16.7 %all-reduce.13.cloned.1.call-done = f32[32,4,128]{2,0,1:T(8,128)} async-done(((f32[32,4,128]{2,0,1:T(8,128)}), f32[32,4,128]{2,0,1:T(8,128)}) %all-reduce.13.cloned.1.call-update) | async-done | bytes 65552 | tf_op jit(solution)/shard_map/psum | solution.py:142
  381.9 42.0 %all-reduce = (f32[32,4]{0,1:T(4,128)S(1)}, f32[32,4]{0,1:T(4,128)S(1)}) all-reduce(f32[32,4]{0,1:T(4,128)S(1)} %get-tuple-element.10, f32[32,4]{0,1:T(4,128)S(1)} %get-tuple-element.9), channel_id=1, replica_groups=mesh['seq'=16,'mdl'=2] {'seq'}, use_global_device_ids=true, to_apply=%region_18.19 | all-reduce | flops 256 | bytes 2048 | tf_op jit(solution)/shard_map/psum | solution.py:143
  423.9 2.7 fusion.31
  426.6 1.8 fusion.29
  428.5 1.5 copy-done.3
  430.1 3.8 convert_select_fusion
  433.8 2.6 convert_select_fusion.1
  436.5 156.9 %all-reduce.15.cloned.1.call-done = (f32[32,4,4096]{2,0,1:T(8,128)}, f32[32,4,4096]{2,0,1:T(8,128)}) async-done(((f32[32,4,4096]{2,0,1:T(8,128)}, f32[32,4,4096]{2,0,1:T(8,128)}), (f32[32,4,4096]{2,0,1:T(8,128)}, f32[32,4,4096]{2,0,1:T(8,128)})) %all-reduce.15.cloned.1.call-update) | async-done | bytes 4194320 | tf_op jit(solution)/shard_map/psum | solution.py:151
  593.3 2.9 fusion.27
  596.2 1.9 all-gather
  (77 shorter events, 8.8 us)
Async XLA Ops:
  7.2 416.7 %copy-start = (bf16[128,4096]{1,0:T(8,128)(2,1)S(1)}, bf16[128,4096]{1,0:T(8,128)(2,1)}, u32[]{:S(2)}) copy-start(bf16[128,4096]{1,0:T(8,128)(2,1)} %param.19) | copy-start | bytes 3145732
  7.2 47.1 %copy-start.1 = (bf16[32,4,128]{2,1,0:T(4,128)(2,1)S(1)}, bf16[32,4,128]{2,1,0:T(4,128)(2,1)}, u32[]{:S(2)}) copy-start(bf16[32,4,128]{2,1,0:T(4,128)(2,1)} %param.11) | copy-start | bytes 98308
  7.2 47.1 %copy-start.14 = (bf16[128,1024]{1,0:T(8,128)(2,1)S(1)}, bf16[128,1024]{1,0:T(8,128)(2,1)}, u32[]{:S(2)}) copy-start(bf16[128,1024]{1,0:T(8,128)(2,1)} %param.16) | copy-start | bytes 786436
  7.2 151.3 %all-reduce.11.cloned.1.call-start = ((), (), s32[]{:S(2)}) async-start(), calls=%async_computation | async-start | bytes 1048576 | tf_op jit(solution)/shard_map/psum | solution.py:81
  53.1 2.8 copy-start.19
  54.2 302.3 %all-reduce.17.cloned.1.call-start = ((), (), s32[]{:S(2)}) async-start(), calls=%async_computation.3 | async-start | bytes 2097152 | tf_op jit(solution)/shard_map/psum | solution.py:109
  56.5 107.7 %copy-start.10 = (f32[32,4,64]{2,1,0:T(4,128)}, f32[32,4,64]{2,1,0:T(4,128)S(1)}, u32[]{:S(2)}) copy-start(f32[32,4,64]{2,1,0:T(4,128)S(1)} %get-tuple-element.32) | copy-start | bytes 98308
  56.5 107.7 %copy-start.12 = (f32[32,4,64]{2,1,0:T(4,128)}, f32[32,4,64]{2,1,0:T(4,128)S(1)}, u32[]{:S(2)}) copy-start(f32[32,4,64]{2,1,0:T(4,128)S(1)} %get-tuple-element.33) | copy-start | bytes 98308
  160.2 4.0 copy-start.16
  160.2 4.0 copy-start.18
  160.3 82.1 %copy-start.2 = (bf16[32,32,1024]{2,1,0:T(8,128)(2,1)S(1)}, bf16[32,32,1024]{2,1,0:T(8,128)(2,1)}, u32[]{:S(2)}) copy-start(bf16[32,32,1024]{2,1,0:T(8,128)(2,1)} %param.13) | copy-start | bytes 6291460
  246.1 110.5 %copy-start.11 = (f32[32,4,64]{2,1,0:T(4,128)S(1)}, f32[32,4,64]{2,1,0:T(4,128)}, u32[]{:S(2)}) copy-start(f32[32,4,64]{2,1,0:T(4,128)} %copy-done.10) | copy-start | bytes 98308
  246.1 110.5 %copy-start.13 = (f32[32,4,64]{2,1,0:T(4,128)S(1)}, f32[32,4,64]{2,1,0:T(4,128)}, u32[]{:S(2)}) copy-start(f32[32,4,64]{2,1,0:T(4,128)} %copy-done.12) | copy-start | bytes 98308
  246.1 112.2 %copy-start.17 = (bf16[32,4,8,64]{3,1,2,0:T(4,128)(2,1)S(1)}, bf16[32,4,8,64]{3,1,2,0:T(4,128)(2,1)}, u32[]{:S(2)}) copy-start(bf16[32,4,8,64]{3,1,2,0:T(4,128)(2,1)} %copy-done.16) | copy-start | bytes 393220
  246.1 134.8 %all-reduce.13.cloned.1.call-start = ((), (), s32[]{:S(2)}) async-start(), calls=%async_computation.1 | async-start | bytes 131072 | tf_op jit(solution)/shard_map/psum | solution.py:142
  329.5 33.5 %copy-start.9 = (bf16[32,4,1024]{2,0,1:T(8,128)(2,1)}, bf16[32,4,1024]{2,0,1:T(8,128)(2,1)S(1)}, u32[]{:S(2)}) copy-start(bf16[32,4,1024]{2,0,1:T(8,128)(2,1)S(1)} %get-tuple-element.15) | copy-start | bytes 786436
  358.3 2.7 copy-start.7
  358.3 2.7 copy-start.21
  363.2 63.4 %copy-start.6 = (bf16[128,4096]{1,0:T(8,128)(2,1)S(1)}, bf16[128,4096]{1,0:T(8,128)(2,1)}, u32[]{:S(2)}) copy-start(bf16[128,4096]{1,0:T(8,128)(2,1)} %param.20) | copy-start | bytes 3145732
  364.1 229.2 %all-reduce.15.cloned.1.call-start = ((), (), s32[]{:S(2)}) async-start(), calls=%async_computation.2 | async-start | bytes 8388608 | tf_op jit(solution)/shard_map/psum | solution.py:151
  380.9 45.7 %copy-start.5 = (f32[32,4,128]{2,0,1:T(8,128)S(1)}, f32[32,4,128]{2,0,1:T(8,128)}, u32[]{:S(2)}) copy-start(f32[32,4,128]{2,0,1:T(8,128)} %all-reduce.13.cloned.1.call-done) | copy-start | bytes 196612
  430.1 3.8 copy-start.4
  430.1 3.8 copy-start.8
  433.8 159.5 %copy-start.20 = (bf16[4096,128]{1,0:T(8,128)(2,1)S(1)}, bf16[4096,128]{1,0:T(8,128)(2,1)}, u32[]{:S(2)}) copy-start(bf16[4096,128]{1,0:T(8,128)(2,1)} %param.21) | copy-start | bytes 3145732
  (2 other events, 3.9 us)
Sparse Core Ops, SparseCore 0:
  54.3 104.1 all-reduce.10
  246.2 110.2 all-reduce.16
  364.2 16.6 all-reduce.12
  428.5 164.7 all-reduce.14
